TPU v7x, 32 devices: a whole 2x2x4 slice. The times are simulated.
32 devices in a mesh: row: 8 (over z, y), col: 4 (over x, core).
Axes of the slice: x: 2, y: 2, z: 4, core: 2. Of those that a mesh axis runs over, the one named last changes fastest.
Arguments:
- points: bfloat16 [4096, 768], P(('row', 'col')), may hold values from -100 to 100
- labels: int32 [4096], P(('row', 'col')), may hold values from 0 to 99
- projection: bfloat16 [256, 768], replicated, may hold values from -0.015625 to 0.015625
Outputs:
- gradient: float32 [256, 768], P('row', 'col')
- class_prob: float32 [4096], P(('row', 'col'))
All inputs are finite; a program needn't handle non-finite values.
Results may differ from a plain program's by a relative error of at most 0.00081.
Values may be sent and summed in bfloat16 or wider, within the bound.
No kernel may reach another device: no remote copies, remote signals or barrier semaphores. Data moves between devices by JAX's collectives and lax.ppermute only.
A program may use at most 64 MiB of HBM per device.

v0:
```python
import jax
import jax.numpy as jnp
from jax import lax
from jax.sharding import PartitionSpec as P


def embed_rows(features, projection):
    return jnp.dot(features, projection.T, preferred_element_type=jnp.float32).astype(jnp.bfloat16)


def split_product(pull, features):
    pull_high = pull.astype(jnp.bfloat16)
    pull_low = (pull - pull_high.astype(jnp.float32)).astype(jnp.bfloat16)
    result = jnp.dot(pull_high.T, features, preferred_element_type=jnp.float32)
    return result + jnp.dot(pull_low.T, features, preferred_element_type=jnp.float32)


def shards(points, labels, projection):
    col_devs = lax.axis_size("col")
    row_devs = lax.axis_size("row")
    row_pos = lax.axis_index("row")
    col_pos = lax.axis_index("col")
    per_device = points.shape[0]
    label_wire = labels.astype(jnp.bfloat16)
    row_feat, row_lab = (
        lax.all_gather(points, "col", axis=0, tiled=True),
        lax.all_gather(label_wire, "col", axis=0, tiled=True),
    )
    col_feat, col_lab = (
        lax.all_gather(points, "row", axis=0, tiled=True),
        lax.all_gather(label_wire, "row", axis=0, tiled=True),
    )
    row_proj = embed_rows(row_feat, projection)
    col_proj = embed_rows(col_feat, projection)
    row_total = row_proj.shape[0]
    col_total = col_proj.shape[0]
    width = row_proj.shape[1]
    row_ids = row_pos * (col_devs * per_device) + jnp.arange(row_total, dtype=jnp.int32)
    col_range = jnp.arange(col_total, dtype=jnp.int32)
    col_ids = (col_range // per_device * col_devs + col_pos) * per_device + col_range % per_device
    row_norm = jnp.sum(jnp.square(row_proj.astype(jnp.float32)), axis=1)
    col_norm = jnp.sum(jnp.square(col_proj.astype(jnp.float32)), axis=1)
    blocksz = min(512, row_total)
    count = row_total // blocksz
    block_proj = row_proj.reshape(count, blocksz, width)
    block_norm = row_norm.reshape(count, blocksz)
    block_ids = row_ids.reshape(count, blocksz)
    block_lab = row_lab.reshape(count, blocksz)

    def scores(rows_proj, rows_norm, rows_ids):
        inner = jnp.dot(rows_proj, col_proj.T, preferred_element_type=jnp.float32)
        value = -(rows_norm[:, None] + col_norm[None, :] - 2.0 * inner)
        return jnp.where(rows_ids[:, None] == col_ids[None, :], -jnp.inf, value)

    def first_pass(items):
        rows_proj, rows_norm, rows_ids, rows_lab = items
        value = scores(rows_proj, rows_norm, rows_ids)
        top = jnp.max(value, axis=1)
        expo = jnp.exp(value - top[:, None])
        match = rows_lab[:, None] == col_lab[None, :]
        return (top, jnp.sum(expo, axis=1), jnp.sum(jnp.where(match, expo, 0.0), axis=1))

    local_top, local_total, local_same = lax.map(
        first_pass, (block_proj, block_norm, block_ids, block_lab)
    )
    local_top = local_top.reshape(row_total)
    local_total = local_total.reshape(row_total)
    local_same = local_same.reshape(row_total)
    top = lax.pmax(local_top, "col")
    factor = jnp.exp(local_top - top)
    total, same = lax.psum((local_total * factor, local_same * factor), "col")
    class_prob = same / total

    def second_pass(carry, items):
        col_sum, wtz = carry
        rows_proj, rows_norm, rows_ids, rows_lab, rows_top, rows_total, rows_prob = items
        value = scores(rows_proj, rows_norm, rows_ids)
        pick = jnp.exp(value - rows_top[:, None]) / rows_total[:, None]
        match = (rows_lab[:, None] == col_lab[None, :]).astype(jnp.float32)
        weight = (pick * (rows_prob[:, None] - match)).astype(jnp.bfloat16)
        weight_f = weight.astype(jnp.float32)
        row_sum = jnp.sum(weight_f, axis=1)
        pull_rows = rows_proj.astype(jnp.float32) * row_sum[:, None] - jnp.dot(
            weight, col_proj, preferred_element_type=jnp.float32
        )
        col_sum = col_sum + jnp.sum(weight_f, axis=0)
        wtz = wtz + jnp.dot(weight.T, rows_proj, preferred_element_type=jnp.float32)
        return ((col_sum, wtz), pull_rows)

    start = (jnp.zeros((col_total,), jnp.float32), jnp.zeros((col_total, width), jnp.float32))
    extras = (
        block_proj,
        block_norm,
        block_ids,
        block_lab,
        top.reshape(count, blocksz),
        total.reshape(count, blocksz),
        class_prob.reshape(count, blocksz),
    )
    (col_sum, wtz), pull_rows = lax.scan(second_pass, start, extras)
    pull_first = pull_rows.reshape(row_total, width)
    pull_second = col_proj.astype(jnp.float32) * col_sum[:, None] - wtz
    partial_value = split_product(pull_first, row_feat) + split_product(pull_second, col_feat)
    summed = lax.psum(partial_value, ("row", "col"))
    rows_each = summed.shape[0] // row_devs
    cols_each = summed.shape[1] // col_devs
    summed = lax.dynamic_slice_in_dim(summed, row_pos * rows_each, rows_each, 0)
    summed = lax.dynamic_slice_in_dim(summed, col_pos * cols_each, cols_each, 1)
    gradient = 2.0 * summed
    own_prob = lax.dynamic_slice_in_dim(class_prob, col_pos * per_device, per_device, 0)
    return (gradient, own_prob)


def solution(mesh):
    in_specs = (P(("row", "col"), None), P(("row", "col")), P())
    out_specs = (P("row", "col"), P(("row", "col")))
    return jax.shard_map(shards, mesh=mesh, in_specs=in_specs, out_specs=out_specs, check_vma=False)
```

profile of v0, /device:TPU:0, one launch (start us, length us, event | category | flops | bytes accessed | tf_op | source)
XLA Modules:
  0.0 218.3 jit_solution(3247269276336462079)
XLA Ops:
  7.2 0.0 copy-start
  7.2 0.0 all-gather.4.cloned.1.call-start
  7.2 0.7 all-gather.4.cloned.1.call-update
  7.9 0.0 all-reduce.3.cloned.1.call-start
  8.0 0.7 convert_bitcast_fusion
  8.6 22.3 %all-gather.1 = bf16[8,1,128]{2,1,0:T(2,128)(2,1)S(1)} all-gather(bf16[1,1,128]{2,1,0:T(2,128)(2,1)S(1)} %convert_bitcast_fusion), channel_id=1, replica_groups=mesh['row'=8,'col'=4] {'row'}, dimensions={0}, use_global_device_ids=true | all-gather | bytes 2304 | tf_op jit(solution)/shard_map/all_gather | solution.py:31
  30.9 5.1 %all-gather = bf16[4,1,128]{2,1,0:T(2,128)(2,1)S(1)} all-gather(bf16[1,1,128]{2,1,0:T(2,128)(2,1)S(1)} %convert_bitcast_fusion), channel_id=1, replica_groups=mesh['row'=8,'col'=4] {'col'}, dimensions={0}, use_global_device_ids=true | all-gather | bytes 1280 | tf_op jit(solution)/shard_map/all_gather | solution.py:27
  36.0 0.6 iota_add_fusion
  36.6 8.9 %all_gather.12 = bf16[512,768]{1,0:T(8,128)(2,1)S(1)} all-gather(bf16[128,768]{1,0:T(8,128)(2,1)} %param.3), channel_id=1, replica_groups=mesh['row'=8,'col'=4] {'col'}, dimensions={0}, use_global_device_ids=true | all-gather | bytes 983040 | tf_op jit(solution)/shard_map/all_gather | solution.py:26
  45.5 0.0 copy-done
  45.5 1.0 fusion.7
  46.5 10.6 %all-gather.4.cloned.1.call-done = bf16[1024,768]{1,0:T(8,128)(2,1)} async-done(((bf16[128,768]{1,0:T(8,128)(2,1)}), bf16[1024,768]{1,0:T(8,128)(2,1)}) %all-gather.4.cloned.1.call-update) | async-done | bytes 1572880 | tf_op jit(solution)/shard_map/all_gather | solution.py:30
  57.1 0.0 copy-start.4
  57.1 2.0 fusion.6
  59.2 0.0 copy-start.2
  59.2 0.0 copy-done.4
  59.2 1.5 fusion.28
  60.7 0.0 copy-done.2
  60.7 5.7 %pmax.7 = f32[512]{0:T(512)S(1)} all-reduce(f32[512]{0:T(512)S(1)} %get-tuple-element.81), channel_id=1, replica_groups=mesh['row'=8,'col'=4] {'col'}, use_global_device_ids=true, to_apply=%region_3.4 | all-reduce | flops 512 | bytes 4096 | tf_op jit(solution)/shard_map/pmax | solution.py:69
  66.3 0.8 fusion.4
  67.1 0.6 fusion.26
  67.7 7.3 %all-reduce = (f32[512]{0:T(512)}, f32[512]{0:T(512)}) all-reduce(f32[512]{0:T(512)} %get-tuple-element.61, f32[512]{0:T(512)} %get-tuple-element.60), channel_id=1, replica_groups=mesh['row'=8,'col'=4] {'col'}, use_global_device_ids=true, to_apply=%region_7.8 | all-reduce | flops 1024 | bytes 8192 | tf_op jit(solution)/shard_map/psum | solution.py:71
  75.0 0.0 copy-start.3
  75.0 0.7 div.27
  75.7 1.7 convert_reduce_fusion
  77.4 0.0 copy-done.3
  77.4 0.5 convolution_subtract_fusion.1
  77.9 0.4 fusion.12
  78.3 0.4 convolution_add_fusion.1
  78.7 0.0 copy-start.1
  78.7 0.5 convolution_subtract_fusion
  79.2 0.9 copy-done.1
  80.1 0.6 fusion.9
  80.7 1.5 fusion.5
  82.2 0.0 all-reduce.3.cloned.1.call-update
  82.2 0.6 dynamic_slice.34
  82.8 127.2 %all-reduce.3.cloned.1.call-done = f32[256,768]{1,0:T(8,128)} async-done(((f32[256,768]{1,0:T(8,128)}), f32[256,768]{1,0:T(8,128)}) %all-reduce.3.cloned.1.call-update) | async-done | bytes 786448 | tf_op jit(solution)/shard_map/psum | solution.py:104
  209.9 1.5 dynamic-slice_multiply_fusion
  (3 shorter events, 0.1 us)
Async XLA Ops:
  7.2 38.4 %copy-start = (bf16[256,768]{1,0:T(8,128)(2,1)S(1)}, bf16[256,768]{1,0:T(8,128)(2,1)}, u32[]{:S(2)}) copy-start(bf16[256,768]{1,0:T(8,128)(2,1)} %param.5) | copy-start | bytes 1179652
  7.2 49.9 %all-gather.4.cloned.1.call-start = ((), (), s32[]{:S(2)}) async-start(), calls=%async_computation | async-start | bytes 1769472 | tf_op jit(solution)/shard_map/all_gather | solution.py:30
  7.9 202.0 %all-reduce.3.cloned.1.call-start = ((), (), s32[]{:S(2)}) async-start(), calls=%async_computation.1 | async-start | bytes 1572864 | tf_op jit(solution)/shard_map/psum | solution.py:104
  57.1 2.1 copy-start.4
  59.2 1.5 copy-start.2
  75.0 2.5 %copy-start.3 = (bf16[1024,256]{0,1:T(8,128)(2,1)S(1)}, bf16[1024,256]{0,1:T(8,128)(2,1)}, u32[]{:S(2)}) copy-start(bf16[1024,256]{0,1:T(8,128)(2,1)} %copy-done.2) | copy-start | bytes 1572868
  78.7 1.4 copy-start.1
Sparse Core Ops, SparseCore 0:
  10.2 46.9 all-gather.3
  82.3 127.5 all-reduce.2
where the time goes:
time: 219 us; the launch traced here: 218 us
  waiting for transfers between devices  138 us (63%)
  blocking collectives  49.2 us (22%)
  between operations  14.2 us (6%)
  matrix products  8.26 us (4%)
  other arithmetic  6.66 us (3%)
    psum x1, waiting for transfers between devices, shards(): summed = lax.psum(partial_value, ('row', 'col'))  127 us
    all_gather x1, blocking collectives, shards(): lax.all_gather(label_wire, 'row', axis=0, tiled=True)  22.3 us
    all_gather x1, waiting for transfers between devices, shards(): lax.all_gather(points, 'row', axis=0, tiled=True)  10.6 us
    all_gather x1, blocking collectives, shards(): lax.all_gather(points, 'col', axis=0, tiled=True)  8.9 us
    psum x1, blocking collectives, shards(): total, same = lax.psum((local_total * factor, local_same * factor), 'col')  7.26 us
    pmax x1, blocking collectives, shards(): top = lax.pmax(local_top, 'col')  5.67 us
    all_gather x1, blocking collectives, shards(): lax.all_gather(label_wire, 'col', axis=0, tiled=True)  5.06 us
  transfers between devices with their start and end apart: 2, of which 2 were waited for; matrix products, arithmetic and copies ran while one was open for 1% of the time, Pallas kernels for 0%

commit v1 on v0

--- a/solution.py
+++ b/solution.py
@@ -2,6 +2,10 @@
 import jax.numpy as jnp
 from jax import lax
 from jax.sharding import PartitionSpec as P
+
+settle_view_for = lambda in_array, dim_k: jnp.concatenate(
+    jax.lax.all_to_all(jnp.stack(jax.lax.axis_size("row") * [in_array]), "row", 0, 0), dim_k
+)
 
 
 def embed_rows(features, projection):
@@ -28,7 +32,7 @@
     )
     col_feat, col_lab = (
         lax.all_gather(points, "row", axis=0, tiled=True),
-        lax.all_gather(label_wire, "row", axis=0, tiled=True),
+        settle_view_for(label_wire, 0),
     )
     row_proj = embed_rows(row_feat, projection)
     col_proj = embed_rows(col_feat, projection)

time: 219 us -> 218 us (level)
  blocking collectives: 49.2 us -> 26.8 us
  waiting for transfers between devices: 138 us -> 153 us
  starting transfers between devices: 0.08 us -> 7.38 us
    all_gather x1 -> x0, blocking collectives: 22.3 us -> none  [shards(): lax.all_gather(label_wire, 'row', axis=0, tiled=True)]
    all_gather x1, waiting for transfers between devices: 10.6 us -> 25 us  [shards(): lax.all_gather(points, 'row', axis=0, tiled=True)]
    all_to_all x0 -> x1, starting transfers between devices: none -> 7.31 us  [jax.lax.all_to_all(jnp.stack(jax.lax.axis_size('row') * [in_array]), 'row...]
  transfers between devices with their start and end apart: 2 -> 3, of which waited for: 2 -> 2; matrix products, arithmetic and copies ran while one was open for 1% -> 2% of each run, Pallas kernels for 0% -> 0%
where the time goes in v1:
time: 218 us
  waiting for transfers between devices  153 us (70%)
  blocking collectives  26.8 us (12%)
  between operations  14.2 us (7%)
  matrix products  7.59 us (3%)
  starting transfers between devices  7.38 us (3%)
  other arithmetic  6.64 us (3%)
    psum x1, waiting for transfers between devices, shards(): summed = lax.psum(partial_value, ('row', 'col'))  127 us
    all_gather x1, waiting for transfers between devices, shards(): lax.all_gather(points, 'row', axis=0, tiled=True)  25 us
    all_gather x1, blocking collectives, shards(): lax.all_gather(points, 'col', axis=0, tiled=True)  8.81 us
    all_to_all x1, starting transfers between devices, jax.lax.all_to_all(jnp.stack(jax.lax.axis_size('row') * [in_array]), 'row...  7.31 us
    psum x1, blocking collectives, shards(): total, same = lax.psum((local_total * factor, local_same * factor), 'col')  7.27 us
    pmax x1, blocking collectives, shards(): top = lax.pmax(local_top, 'col')  5.66 us
    all_gather x1, blocking collectives, shards(): lax.all_gather(label_wire, 'col', axis=0, tiled=True)  5.05 us
  transfers between devices with their start and end apart: 3, of which 2 were waited for; matrix products, arithmetic and copies ran while one was open for 2% of the time, Pallas kernels for 0%

profile of v1, /device:TPU:0, one launch (start us, length us, event | category | flops | bytes accessed | tf_op | source)
XLA Modules:
  0.0 217.7 jit_solution(2469459841967580081)
XLA Ops:
  7.2 0.0 copy-start
  7.2 0.0 all-gather.3.cloned.1.call-start
  7.2 0.7 all-gather.3.cloned.1.call-update
  7.9 0.7 convert_bitcast_fusion
  8.6 0.6 stack.2
  9.2 7.3 %all-to-all-start = ((bf16[8,1,128]{2,1,0:T(2,128)(2,1)}), bf16[8,1,128]{2,1,0:T(2,128)(2,1)S(1)}, u32[]{:S(2)}, u32[]{:S(2)}) async-start(bf16[8,1,128]{2,1,0:T(2,128)(2,1)} %stack.2), calls=%async_computation | async-start | bytes 8192 | tf_op jit(solution)/shard_map/all_to_all | solution.py:7
  16.5 0.0 all-reduce.3.cloned.1.call-start
  16.5 8.8 %all_gather.9 = bf16[512,768]{1,0:T(8,128)(2,1)S(1)} all-gather(bf16[128,768]{1,0:T(8,128)(2,1)} %param.3), channel_id=1, replica_groups=mesh['row'=8,'col'=4] {'col'}, dimensions={0}, use_global_device_ids=true | all-gather | bytes 983040 | tf_op jit(solution)/shard_map/all_gather | solution.py:30
  25.4 0.0 copy-done
  25.4 1.0 fusion.7
  26.4 0.6 iota_add_fusion
  26.9 5.0 %all-gather = bf16[4,1,128]{2,1,0:T(2,128)(2,1)S(1)} all-gather(bf16[1,1,128]{2,1,0:T(2,128)(2,1)S(1)} %get-tuple-element.62), channel_id=1, replica_groups=mesh['row'=8,'col'=4] {'col'}, dimensions={0}, use_global_device_ids=true | all-gather | bytes 1280 | tf_op jit(solution)/shard_map/all_gather | solution.py:31
  32.0 0.0 all-to-all-done
  32.0 25.0 %all-gather.3.cloned.1.call-done = bf16[1024,768]{1,0:T(8,128)(2,1)} async-done(((bf16[128,768]{1,0:T(8,128)(2,1)}), bf16[1024,768]{1,0:T(8,128)(2,1)}) %all-gather.3.cloned.1.call-update) | async-done | bytes 1572880 | tf_op jit(solution)/shard_map/all_gather | solution.py:34
  57.1 0.0 copy-start.4
  57.1 0.0 copy-start.5
  57.1 2.0 fusion.6
  59.1 0.0 copy-start.2
  59.1 0.0 copy-done.4
  59.1 0.0 copy-done.5
  59.1 0.8 fusion.28
  59.9 0.0 copy-done.2
  59.9 5.7 %pmax.7 = f32[512]{0:T(512)S(1)} all-reduce(f32[512]{0:T(512)S(1)} %get-tuple-element.83), channel_id=1, replica_groups=mesh['row'=8,'col'=4] {'col'}, use_global_device_ids=true, to_apply=%region_3.4 | all-reduce | flops 512 | bytes 4096 | tf_op jit(solution)/shard_map/pmax | solution.py:73
  65.6 0.8 fusion.4
  66.3 0.6 fusion.26
  66.9 7.3 %all-reduce = (f32[512]{0:T(512)}, f32[512]{0:T(512)}) all-reduce(f32[512]{0:T(512)} %get-tuple-element.61, f32[512]{0:T(512)} %get-tuple-element.60), channel_id=1, replica_groups=mesh['row'=8,'col'=4] {'col'}, use_global_device_ids=true, to_apply=%region_7.8 | all-reduce | flops 1024 | bytes 8192 | tf_op jit(solution)/shard_map/psum | solution.py:75
  74.2 0.0 copy-start.3
  74.2 0.7 div.27
  75.0 1.7 convert_reduce_fusion
  76.7 0.0 copy-done.3
  76.7 0.5 convolution_subtract_fusion.1
  77.2 0.4 fusion.12
  77.6 0.4 convolution_add_fusion.1
  77.9 0.0 copy-start.1
  78.0 0.5 convolution_subtract_fusion
  78.4 0.9 copy-done.1
  79.4 0.6 fusion.9
  79.9 1.5 fusion.5
  81.4 0.0 all-reduce.3.cloned.1.call-update
  81.5 0.6 dynamic_slice.34
  82.1 127.2 %all-reduce.3.cloned.1.call-done = f32[256,768]{1,0:T(8,128)} async-done(((f32[256,768]{1,0:T(8,128)}), f32[256,768]{1,0:T(8,128)}) %all-reduce.3.cloned.1.call-update) | async-done | bytes 786448 | tf_op jit(solution)/shard_map/psum | solution.py:108
  209.3 1.5 dynamic-slice_multiply_fusion
  (3 shorter events, 0.1 us)
Async XLA Ops:
  7.2 18.2 %copy-start = (bf16[256,768]{1,0:T(8,128)(2,1)S(1)}, bf16[256,768]{1,0:T(8,128)(2,1)}, u32[]{:S(2)}) copy-start(bf16[256,768]{1,0:T(8,128)(2,1)} %param.5) | copy-start | bytes 1179652
  7.2 49.9 %all-gather.3.cloned.1.call-start = ((), (), s32[]{:S(2)}) async-start(), calls=%async_computation.1 | async-start | bytes 1769472 | tf_op jit(solution)/shard_map/all_gather | solution.py:34
  9.2 22.8 %all-to-all-start = ((bf16[8,1,128]{2,1,0:T(2,128)(2,1)}), bf16[8,1,128]{2,1,0:T(2,128)(2,1)S(1)}, u32[]{:S(2)}, u32[]{:S(2)}) async-start(bf16[8,1,128]{2,1,0:T(2,128)(2,1)} %stack.2), calls=%async_computation | async-start | bytes 8192 | tf_op jit(solution)/shard_map/all_to_all | solution.py:7
  16.5 192.8 %all-reduce.3.cloned.1.call-start = ((), (), s32[]{:S(2)}) async-start(), calls=%async_computation.2 | async-start | bytes 1572864 | tf_op jit(solution)/shard_map/psum | solution.py:108
  57.1 2.0 copy-start.4
  57.1 2.1 copy-start.5
  59.1 0.8 copy-start.2
  74.2 2.5 %copy-start.3 = (bf16[1024,256]{0,1:T(8,128)(2,1)S(1)}, bf16[1024,256]{0,1:T(8,128)(2,1)}, u32[]{:S(2)}) copy-start(bf16[1024,256]{0,1:T(8,128)(2,1)} %copy-done.2) | copy-start | bytes 1572868
  77.9 1.4 copy-start.1
Sparse Core Ops, SparseCore 0:
  10.2 46.8 all-gather.2
  81.6 127.6 all-reduce.2
